TPU v7x, 32 devices: a whole 2x2x4 slice. The times are simulated.
32 devices in a mesh: row: 8 (over y, x, core), col: 4 (over z).
Axes of the slice: x: 2, y: 2, z: 4, core: 2. Of those that a mesh axis runs over, the one named last changes fastest.
Arguments:
- tiles: bfloat16 [8, 64, 128, 128], P('row', 'col'), may hold values from -2 to 2
- tile_index: int32 [8, 64], P('row', 'col'), may hold values from 0 to 16384, as said below
- u_basis: float32 [64, 131072], P(None, ('row', 'col')), may hold values from -10 to 10
- v_basis: float32 [64, 4, 16384], P(None, 'col', 'row'), may hold values from -10 to 10
- v_start: float32 [65536], P('col'), may hold values from -0.5 to 1.5
Outputs:
- left_vectors: float32 [2, 131072], P(None, ('row', 'col'))
- right_vectors: float32 [2, 4, 16384], P(None, 'col', 'row')
- bidiagonal: float32 [2, 2], replicated
Inputs may be any that keep to these rules, and one draw needn't show every extreme that they name: `tile_index`: each block's 16 slots name distinct tiles of its 128 x 128 block as r * 128 + c; the value 128 * 128 marks an empty slot, and empty slots come after all live ones. Blocks have different numbers of live slots, at least 4; some block has all 16 slots live.
All inputs are finite; a program needn't handle non-finite values.
Results may differ from a plain program's by a relative error of at most 0.0003.
Values sent between devices are 32-bit elements; how exact they have to be, the bound alone decides.
No kernel may reach another device: no remote copies, remote signals or barrier semaphores. Data moves between devices by JAX's collectives and lax.ppermute only.
A program may use at most 64 MiB of HBM per device.

v0:
```python
import jax
import jax.numpy as jnp
from jax import lax
from jax.sharding import PartitionSpec as P

ITERS = 2
HIGHEST = lax.Precision.HIGHEST
EPSILON = 1e-06


def project_gram(share, basis, gram, total):
    coeffs, squares = lax.psum(
        (jnp.dot(basis, share, precision=HIGHEST), jnp.sum(share * share)), ("row", "col")
    )
    coeffs = coeffs / total
    squares = squares / total
    second = coeffs - jnp.dot(gram, coeffs, precision=HIGHEST)
    combined = coeffs + second
    gram_comb = jnp.dot(gram, combined, precision=HIGHEST)
    remaining = coeffs - gram_comb
    squared = (
        squares
        - 2.0 * jnp.dot(combined, coeffs, precision=HIGHEST)
        + jnp.dot(combined, gram_comb, precision=HIGHEST)
    )
    scale = jnp.sqrt(squared + EPSILON)
    unit = (share - jnp.dot(combined, basis, precision=HIGHEST)) / scale
    column = remaining / scale
    corner = squared / (scale * scale)
    upper = jnp.concatenate([gram, column[:, None]], 1)
    lower = jnp.concatenate([column, corner[None]])[None, :]
    return (unit, scale, jnp.concatenate([upper, lower], 0), combined)


def shards(tiles, tile_index, u_basis, v_basis, v_start):
    blocks = tiles[0].astype(jnp.float32)
    slots = tile_index[0]
    width = blocks.shape[1]
    cols_len = v_start.shape[0]
    col_blocks = cols_len // width
    row_count = lax.axis_size("row")
    col_count = lax.axis_size("col")
    left_piece = u_basis.shape[1]
    right_piece = v_basis.shape[2]
    rows_len = left_piece * col_count
    row_blocks = rows_len // width
    total_left = rows_len * row_count
    total_right = cols_len * col_count
    rows_hot = (slots[:, None] // col_blocks == jnp.arange(row_blocks)[None, :]).astype(jnp.float32)
    cols_hot = (slots[:, None] % col_blocks == jnp.arange(col_blocks)[None, :]).astype(jnp.float32)
    left_start = lax.axis_index("col") * left_piece
    right_start = lax.axis_index("row") * right_piece

    def forward_many(vectors):
        count = vectors.shape[0]
        picked = jnp.einsum(
            "tc,mck->mtk", cols_hot, vectors.reshape(count, col_blocks, width), precision=HIGHEST
        )
        product = jnp.einsum("tab,mtb->mta", blocks, picked, precision=HIGHEST)
        return jnp.einsum("tr,mta->mra", rows_hot, product, precision=HIGHEST).reshape(
            count, rows_len
        )

    def forward(vector):
        return forward_many(vector[None, :])[0]

    left_basis = u_basis
    start_share = lax.dynamic_slice_in_dim(v_start, right_start, right_piece)
    right_basis = jnp.concatenate([v_basis[:, 0, :], start_share[None, :]], 0)
    left_gram, right_gram = lax.psum(
        (
            jnp.dot(left_basis, left_basis.T, precision=HIGHEST),
            jnp.dot(right_basis, right_basis.T, precision=HIGHEST),
        ),
        ("row", "col"),
    )
    left_gram = left_gram / total_left
    right_gram = right_gram / total_right
    forward_now = forward(v_start)
    lefts, rights, alphas, betas = ([], [], [], [])
    for iteration in range(ITERS):
        left_whole = lax.psum(forward_now, "col")
        left_result = lax.dynamic_slice_in_dim(left_whole, left_start, left_piece)
        share = left_result
        left_unit, alpha, left_gram, combined = project_gram(
            share, left_basis, left_gram, total_left
        )
        left_basis = jnp.concatenate([left_basis, left_unit[None, :]], 0)
        join_joined = lax.all_gather(left_unit, "col", axis=0, tiled=True)
        backward_vectors = join_joined[None, :]
        backward_count = backward_vectors.shape[0]
        backward_picked = jnp.einsum(
            "tr,mrk->mtk",
            rows_hot,
            backward_vectors.reshape(backward_count, row_blocks, width),
            precision=HIGHEST,
        )
        backward_product = jnp.einsum("tab,mta->mtb", blocks, backward_picked, precision=HIGHEST)
        backward_now = jnp.einsum(
            "tc,mtb->mcb", cols_hot, backward_product, precision=HIGHEST
        ).reshape(backward_count, cols_len)[0]
        whole = lax.psum(backward_now, "row")
        result = lax.dynamic_slice_in_dim(whole, right_start, right_piece)
        share = result
        right_unit, beta, right_gram, combined = project_gram(
            share, right_basis, right_gram, total_right
        )
        right_basis = jnp.concatenate([right_basis, right_unit[None, :]], 0)
        if iteration + 1 < ITERS:
            joined = lax.all_gather(right_unit, "row", axis=0, tiled=True)
            forward_now = forward(joined)
        lefts.append(left_unit)
        rights.append(right_unit)
        alphas.append(alpha)
        betas.append(beta)
    left_vectors = jnp.stack(lefts)
    right_vectors = jnp.stack(rights)[:, None, :]
    bidiagonal = jnp.stack([jnp.stack(alphas), jnp.stack(betas)])
    return (left_vectors, right_vectors, bidiagonal)


def solution(mesh):
    placed = (
        P("row", "col", None, None),
        P("row", "col"),
        P(None, ("row", "col")),
        P(None, "col", "row"),
        P("col"),
    )
    return jax.shard_map(
        shards,
        mesh=mesh,
        in_specs=placed,
        out_specs=(P(None, ("row", "col")), P(None, "col", "row"), P()),
        check_vma=False,
    )
```

profile of v0, /device:TPU:0, one launch (start us, length us, event | category | flops | bytes accessed | tf_op | source)
XLA Modules:
  0.0 422.3 jit_solution(5851223043497568862)
XLA Ops:
  7.9 1.0 fusion.30
  9.0 0.9 fusion.19
  11.0 2.8 fusion.72
  15.4 32.7 %all-reduce.9.cloned.1.call-done = f32[16384]{0:T(1024)} async-done(((f32[16384]{0:T(1024)}), f32[16384]{0:T(1024)}) %all-reduce.9.cloned.1.call-update) | async-done | bytes 65552 | tf_op jit(solution)/shard_map/psum | solution.py:82
  48.1 1.3 multiply_reduce_fusion.1
  49.4 0.9 convolution_bitcast_fusion.5
  50.3 40.5 %all-reduce.3 = (f32[64]{0:T(128)S(1)}, f32[64,64]{1,0:T(8,128)S(1)}, f32[]{:T(128)}) all-reduce(f32[64]{0:T(128)S(1)} %convolution_bitcast_fusion.5, f32[64,64]{1,0:T(8,128)S(1)} %fusion.72, f32[]{:T(128)} %get-tuple-element.23), channel_id=1, replica_groups=mesh['row'=8,'col'=4] {'row','col'}, use_global_device_ids=true, to_apply=%region_1.2 | all-reduce | flops 4161 | bytes 33288 | tf_op jit(solution)/shard_map/psum | solution.py:12
  94.4 13.3 %all_gather.9 = f32[16384]{0:T(1024)S(1)} all-gather(f32[4096]{0:T(1024)S(1)} %subtract_divide_fusion.1), channel_id=1, replica_groups=mesh['row'=8,'col'=4] {'col'}, dimensions={0}, use_global_device_ids=true | all-gather | bytes 81920 | tf_op jit(solution)/shard_map/all_gather | solution.py:89
  109.7 52.5 %all-reduce.11.cloned.1.call-done = f32[16384]{0:T(1024)} async-done(((f32[16384]{0:T(1024)}), f32[16384]{0:T(1024)}) %all-reduce.11.cloned.1.call-update) | async-done | bytes 65552 | tf_op jit(solution)/shard_map/psum | solution.py:102
  162.2 1.3 multiply_reduce_fusion.3
  164.1 39.8 %all-reduce.2 = (f32[65]{0:T(128)S(1)}, f32[65,65]{1,0:T(8,128)S(1)}, f32[]{:T(128)}) all-reduce(f32[65]{0:T(128)S(1)} %convolution_bitcast_fusion.15, f32[65,65]{1,0:T(8,128)S(1)} %fusion.23, f32[]{:T(128)} %get-tuple-element.21), channel_id=1, replica_groups=mesh['row'=8,'col'=4] {'row','col'}, use_global_device_ids=true, to_apply=%region_6.7 | all-reduce | flops 4291 | bytes 34328 | tf_op jit(solution)/shard_map/psum | solution.py:12
  204.5 0.9 multiply_reduce_fusion.6
  207.4 10.0 %all_gather.10 = f32[16384]{0:T(1024)S(1)} all-gather(f32[2048]{0:T(1024)S(1)} %subtract_divide_fusion.3), channel_id=1, replica_groups=mesh['row'=8,'col'=4] {'row'}, dimensions={0}, use_global_device_ids=true | all-gather | bytes 73728 | tf_op jit(solution)/shard_map/all_gather | solution.py:110
  217.6 0.9 fusion.15
  219.8 33.1 %all-reduce.13.cloned.1.call-done = f32[16384]{0:T(1024)} async-done(((f32[16384]{0:T(1024)}), f32[16384]{0:T(1024)}) %all-reduce.13.cloned.1.call-update) | async-done | bytes 65552 | tf_op jit(solution)/shard_map/psum | solution.py:82
  252.9 1.3 multiply_reduce_fusion
  254.3 1.0 convolution_bitcast_fusion.4
  255.3 40.3 %all-reduce.1 = (f32[65]{0:T(128)S(1)}, f32[]{:T(128)}) all-reduce(f32[65]{0:T(128)S(1)} %convolution_bitcast_fusion.4, f32[]{:T(128)} %get-tuple-element.19), channel_id=1, replica_groups=mesh['row'=8,'col'=4] {'row','col'}, use_global_device_ids=true, to_apply=%region_11.12 | all-reduce | flops 66 | bytes 528 | tf_op jit(solution)/shard_map/psum | solution.py:12
  297.1 0.9 fusion.11
  300.1 13.3 %all_gather.11 = f32[16384]{0:T(1024)S(1)} all-gather(f32[4096]{0:T(1024)S(1)} %subtract_divide_fusion), channel_id=1, replica_groups=mesh['row'=8,'col'=4] {'col'}, dimensions={0}, use_global_device_ids=true | all-gather | bytes 81920 | tf_op jit(solution)/shard_map/all_gather | solution.py:89
  315.8 53.1 %all-reduce.15.cloned.1.call-done = f32[16384]{0:T(1024)} async-done(((f32[16384]{0:T(1024)}), f32[16384]{0:T(1024)}) %all-reduce.15.cloned.1.call-update) | async-done | bytes 65552 | tf_op jit(solution)/shard_map/psum | solution.py:102
  368.9 1.3 multiply_reduce_fusion.2
  370.8 39.5 %all-reduce = (f32[66]{0:T(128)S(1)}, f32[]{:T(128)}) all-reduce(f32[66]{0:T(128)S(1)} %convolution_bitcast_fusion.14, f32[]{:T(128)} %get-tuple-element.17), channel_id=1, replica_groups=mesh['row'=8,'col'=4] {'row','col'}, use_global_device_ids=true, to_apply=%region_15.16 | all-reduce | flops 67 | bytes 536 | tf_op jit(solution)/shard_map/psum | solution.py:12
  411.5 0.9 fusion.12
  (60 shorter events, 16.6 us)
Async XLA Ops:
  7.2 1.8 copy-start
  7.2 40.9 %all-reduce.9.cloned.1.call-start = ((), (), s32[]{:S(2)}) async-start(), calls=%async_computation | async-start | bytes 131072 | tf_op jit(solution)/shard_map/psum | solution.py:82
  10.9 151.3 %all-reduce.11.cloned.1.call-start = ((), (), s32[]{:S(2)}) async-start(), calls=%async_computation.1 | async-start | bytes 131072 | tf_op jit(solution)/shard_map/psum | solution.py:102
  11.0 3.6 copy-start.2
  13.8 35.6 %copy-start.1 = (f32[64,4096]{1,0:T(8,128)S(1)}, f32[64,4096]{1,0:T(8,128)}, u32[]{:S(2)}) copy-start(f32[64,4096]{1,0:T(8,128)} %param.7) | copy-start | bytes 3145732
  109.4 143.5 %all-reduce.13.cloned.1.call-start = ((), (), s32[]{:S(2)}) async-start(), calls=%async_computation.2 | async-start | bytes 131072 | tf_op jit(solution)/shard_map/psum | solution.py:82
  219.5 149.4 %all-reduce.15.cloned.1.call-start = ((), (), s32[]{:S(2)}) async-start(), calls=%async_computation.3 | async-start | bytes 131072 | tf_op jit(solution)/shard_map/psum | solution.py:102
Sparse Core Ops, SparseCore 0:
  11.0 37.0 all-reduce.8
  109.5 52.6 all-reduce.10
  219.6 33.2 all-reduce.12
  315.9 52.9 all-reduce.14
where the time goes:
time: 424 us; the launch traced here: 422 us
  blocking collectives  197 us (46%)
  waiting for transfers between devices  171 us (40%)
  between operations  22.1 us (5%)
  matrix products  19.7 us (5%)
  other arithmetic  7.56 us (2%)
  local copies, waits for them, and re-layouts  4.67 us (1%)
    psum x4, blocking collectives, project_gram(): lax.psum((jnp.dot(basis, share, precision=HIGHEST), jnp.sum(share * share...  160 us
    psum x2, waiting for transfers between devices, shards(): whole = lax.psum(backward_now, 'row')  106 us
    psum x2, waiting for transfers between devices, shards(): left_whole = lax.psum(forward_now, 'col')  65.8 us
    all_gather x2, blocking collectives, shards(): join_joined = lax.all_gather(left_unit, 'col', axis=0, tiled=True)  26.6 us
    all_gather x1, blocking collectives, shards(): joined = lax.all_gather(right_unit, 'row', axis=0, tiled=True)  9.99 us
  transfers between devices with their start and end apart: 4, of which 4 were waited for; matrix products, arithmetic and copies ran while one was open for 1% of the time, Pallas kernels for 0%

commit v1 on v0

--- a/solution.py
+++ b/solution.py
@@ -9,9 +9,13 @@
 
 
 def project_gram(share, basis, gram, total):
-    coeffs, squares = lax.psum(
-        (jnp.dot(basis, share, precision=HIGHEST), jnp.sum(share * share)), ("row", "col")
-    )
+
+    def fix_heads(x0):
+        for to_i in ("col", "row"):
+            x0 = jax.lax.psum(x0, to_i)
+        return x0
+
+    coeffs, squares = fix_heads((jnp.dot(basis, share, precision=HIGHEST), jnp.sum(share * share)))
     coeffs = coeffs / total
     squares = squares / total
     second = coeffs - jnp.dot(gram, coeffs, precision=HIGHEST)

time: 424 us -> 363 us (0.86)
  waiting for transfers between devices: 171 us -> 133 us
  blocking collectives: 197 us -> 175 us
    psum x2, waiting for transfers between devices: 65.8 us -> 31.4 us  [shards(): left_whole = lax.psum(forward_now, 'col')]
    psum x4 -> x9, blocking collectives: 160 us -> 140 us  [the longest x8 96.5 us: fix_heads(): x0 = jax.lax.psum(x0, to_i)]
  transfers between devices with their start and end apart: 4 -> 4, of which waited for: 4 -> 3; matrix products, arithmetic and copies ran while one was open for 1% -> 1% of each run, Pallas kernels for 0% -> 0%
where the time goes in v1:
time: 363 us; the launch traced here: 362 us
  blocking collectives  175 us (48%)
  waiting for transfers between devices  133 us (37%)
  between operations  22.1 us (6%)
  matrix products  19.7 us (5%)
  other arithmetic  7.57 us (2%)
  local copies, waits for them, and re-layouts  4.66 us (1%)
    psum x2, waiting for transfers between devices, shards(): whole = lax.psum(backward_now, 'row')  102 us
    psum x8, blocking collectives, fix_heads(): x0 = jax.lax.psum(x0, to_i)  96.5 us
    psum x1, blocking collectives, shards(): lax.psum((jnp.dot(left_basis, left_basis.T, precision=HIGHEST), jnp.dot(r...  43.2 us
    psum x2, waiting for transfers between devices, shards(): left_whole = lax.psum(forward_now, 'col')  31.4 us
    all_gather x2, blocking collectives, shards(): join_joined = lax.all_gather(left_unit, 'col', axis=0, tiled=True)  26.4 us
    all_gather x1, blocking collectives, shards(): joined = lax.all_gather(right_unit, 'row', axis=0, tiled=True)  8.62 us
  transfers between devices with their start and end apart: 4, of which 3 were waited for; matrix products, arithmetic and copies ran while one was open for 1% of the time, Pallas kernels for 0%

profile of v1, /device:TPU:0, one launch (start us, length us, event | category | flops | bytes accessed | tf_op | source)
XLA Modules:
  0.0 362.0 jit_solution(5567283080896087401)
XLA Ops:
  7.9 1.0 fusion.30
  9.0 0.9 fusion.19
  11.0 2.8 fusion.72
  15.4 43.2 %all-reduce = (f32[64,64]{1,0:T(8,128)S(1)}, f32[65,65]{1,0:T(8,128)S(1)}) all-reduce(f32[64,64]{1,0:T(8,128)S(1)} %fusion.72, f32[65,65]{1,0:T(8,128)S(1)} %fusion.23), channel_id=1, replica_groups=mesh['row'=8,'col'=4] {'row','col'}, use_global_device_ids=true, to_apply=%region_3.4 | all-reduce | flops 8321 | bytes 66568 | tf_op jit(solution)/shard_map/psum | solution.py:74
  58.6 1.3 multiply_reduce_fusion.1
  60.9 11.1 %all-reduce.8 = (f32[64]{0:T(128)S(1)}, f32[]{:T(128)}) all-reduce(f32[64]{0:T(128)S(1)} %convolution_bitcast_fusion.5, f32[]{:T(128)} %get-tuple-element.31), channel_id=1, replica_groups=mesh['row'=8,'col'=4] {'col'}, use_global_device_ids=true, to_apply=%region_1.2 | all-reduce | flops 65 | bytes 520 | tf_op jit(solution)/shard_map/psum | solution.py:15
  72.0 12.4 %all-reduce.4 = (f32[64]{0:T(128)S(1)}, f32[]{:T(128)}) all-reduce(f32[64]{0:T(128)S(1)} %get-tuple-element.23, f32[]{:T(128)} %get-tuple-element.24), channel_id=1, replica_groups=mesh['row'=8,'col'=4] {'row'}, use_global_device_ids=true, to_apply=%region_2.3 | all-reduce | flops 65 | bytes 520 | tf_op jit(solution)/shard_map/psum | solution.py:15
  88.0 13.2 %all_gather.9 = f32[16384]{0:T(1024)S(1)} all-gather(f32[4096]{0:T(1024)S(1)} %subtract_divide_fusion.1), channel_id=1, replica_groups=mesh['row'=8,'col'=4] {'col'}, dimensions={0}, use_global_device_ids=true | all-gather | bytes 81920 | tf_op jit(solution)/shard_map/all_gather | solution.py:93
  103.2 51.1 %all-reduce.16.cloned.1.call-done = f32[16384]{0:T(1024)} async-done(((f32[16384]{0:T(1024)}), f32[16384]{0:T(1024)}) %all-reduce.16.cloned.1.call-update) | async-done | bytes 65552 | tf_op jit(solution)/shard_map/psum | solution.py:106
  154.3 1.3 multiply_reduce_fusion.3
  156.2 12.3 %all-reduce.7 = (f32[65]{0:T(128)S(1)}, f32[]{:T(128)}) all-reduce(f32[65]{0:T(128)S(1)} %convolution_bitcast_fusion.15, f32[]{:T(128)} %get-tuple-element.29), channel_id=1, replica_groups=mesh['row'=8,'col'=4] {'col'}, use_global_device_ids=true, to_apply=%region_8.9 | all-reduce | flops 66 | bytes 528 | tf_op jit(solution)/shard_map/psum | solution.py:15
  168.5 12.4 %all-reduce.3 = (f32[65]{0:T(128)S(1)}, f32[]{:T(128)}) all-reduce(f32[65]{0:T(128)S(1)} %get-tuple-element.21, f32[]{:T(128)} %get-tuple-element.22), channel_id=1, replica_groups=mesh['row'=8,'col'=4] {'row'}, use_global_device_ids=true, to_apply=%region_9.10 | all-reduce | flops 66 | bytes 528 | tf_op jit(solution)/shard_map/psum | solution.py:15
  184.4 8.6 %all_gather.10 = f32[16384]{0:T(1024)S(1)} all-gather(f32[2048]{0:T(1024)S(1)} %subtract_divide_fusion.3), channel_id=1, replica_groups=mesh['row'=8,'col'=4] {'row'}, dimensions={0}, use_global_device_ids=true | all-gather | bytes 73728 | tf_op jit(solution)/shard_map/all_gather | solution.py:114
  193.2 0.9 fusion.15
  195.4 31.4 %all-reduce.18.cloned.1.call-done = f32[16384]{0:T(1024)} async-done(((f32[16384]{0:T(1024)}), f32[16384]{0:T(1024)}) %all-reduce.18.cloned.1.call-update) | async-done | bytes 65552 | tf_op jit(solution)/shard_map/psum | solution.py:86
  226.8 1.3 multiply_reduce_fusion
  228.1 1.0 convolution_bitcast_fusion.4
  229.2 11.1 %all-reduce.6 = (f32[65]{0:T(128)S(1)}, f32[]{:T(128)}) all-reduce(f32[65]{0:T(128)S(1)} %convolution_bitcast_fusion.4, f32[]{:T(128)} %get-tuple-element.27), channel_id=1, replica_groups=mesh['row'=8,'col'=4] {'col'}, use_global_device_ids=true, to_apply=%region_15.16 | all-reduce | flops 66 | bytes 528 | tf_op jit(solution)/shard_map/psum | solution.py:15
  240.3 12.4 %all-reduce.2 = (f32[65]{0:T(128)S(1)}, f32[]{:T(128)}) all-reduce(f32[65]{0:T(128)S(1)} %get-tuple-element.19, f32[]{:T(128)} %get-tuple-element.20), channel_id=1, replica_groups=mesh['row'=8,'col'=4] {'row'}, use_global_device_ids=true, to_apply=%region_16.17 | all-reduce | flops 66 | bytes 528 | tf_op jit(solution)/shard_map/psum | solution.py:15
  257.2 13.2 %all_gather.11 = f32[16384]{0:T(1024)S(1)} all-gather(f32[4096]{0:T(1024)S(1)} %subtract_divide_fusion), channel_id=1, replica_groups=mesh['row'=8,'col'=4] {'col'}, dimensions={0}, use_global_device_ids=true | all-gather | bytes 81920 | tf_op jit(solution)/shard_map/all_gather | solution.py:93
  272.8 50.5 %all-reduce.20.cloned.1.call-done = f32[16384]{0:T(1024)} async-done(((f32[16384]{0:T(1024)}), f32[16384]{0:T(1024)}) %all-reduce.20.cloned.1.call-update) | async-done | bytes 65552 | tf_op jit(solution)/shard_map/psum | solution.py:106
  323.4 1.3 multiply_reduce_fusion.2
  325.2 12.3 %all-reduce.5 = (f32[66]{0:T(128)S(1)}, f32[]{:T(128)}) all-reduce(f32[66]{0:T(128)S(1)} %convolution_bitcast_fusion.14, f32[]{:T(128)} %get-tuple-element.25), channel_id=1, replica_groups=mesh['row'=8,'col'=4] {'col'}, use_global_device_ids=true, to_apply=%region_21.22 | all-reduce | flops 67 | bytes 536 | tf_op jit(solution)/shard_map/psum | solution.py:15
  337.5 12.4 %all-reduce.1 = (f32[66]{0:T(128)S(1)}, f32[]{:T(128)}) all-reduce(f32[66]{0:T(128)S(1)} %get-tuple-element.17, f32[]{:T(128)} %get-tuple-element.18), channel_id=1, replica_groups=mesh['row'=8,'col'=4] {'row'}, use_global_device_ids=true, to_apply=%region_22.23 | all-reduce | flops 67 | bytes 536 | tf_op jit(solution)/shard_map/psum | solution.py:15
  (65 shorter events, 20.2 us)
Async XLA Ops:
  7.2 1.8 copy-start
  7.2 51.4 %all-reduce.14.cloned.1.call-start = ((), (), s32[]{:S(2)}) async-start(), calls=%async_computation | async-start | bytes 131072 | tf_op jit(solution)/shard_map/psum | solution.py:86
  10.9 143.4 %all-reduce.16.cloned.1.call-start = ((), (), s32[]{:S(2)}) async-start(), calls=%async_computation.1 | async-start | bytes 131072 | tf_op jit(solution)/shard_map/psum | solution.py:106
  11.0 3.6 %copy-start.2 = (f32[64,1,2048]{2,1,0:T(1,128)S(1)}, f32[64,1,2048]{2,1,0:T(1,128)}, u32[]{:S(2)}) copy-start(f32[64,1,2048]{2,1,0:T(1,128)} %param.8) | copy-start | bytes 1572868
  13.8 46.2 %copy-start.1 = (f32[64,4096]{1,0:T(8,128)S(1)}, f32[64,4096]{1,0:T(8,128)}, u32[]{:S(2)}) copy-start(f32[64,4096]{1,0:T(8,128)} %param.7) | copy-start | bytes 3145732
  102.9 123.9 %all-reduce.18.cloned.1.call-start = ((), (), s32[]{:S(2)}) async-start(), calls=%async_computation.2 | async-start | bytes 131072 | tf_op jit(solution)/shard_map/psum | solution.py:86
  195.1 128.2 %all-reduce.20.cloned.1.call-start = ((), (), s32[]{:S(2)}) async-start(), calls=%async_computation.3 | async-start | bytes 131072 | tf_op jit(solution)/shard_map/psum | solution.py:106
Sparse Core Ops, SparseCore 0:
  11.0 37.0 all-reduce.13
  103.0 51.2 all-reduce.15
  195.3 31.5 all-reduce.17
  272.9 50.4 all-reduce.19
